TPU v7x, 32 devices: a whole 2x2x4 slice. The times are simulated.
32 devices in a mesh: sample: 8 (over y, x, core), chan: 4 (over z).
Axes of the slice: x: 2, y: 2, z: 4, core: 2. Of those that a mesh axis runs over, the one named last changes fastest.
Arguments:
- snapshots: bfloat16 [8, 256, 512], P('sample', None, 'chan'), may hold values from -6 to 6
- first_weight: bfloat16 [256, 27, 256], P('chan'), may hold values from -0.078125 to 0.078125
- second_weight: bfloat16 [256, 27, 256], P('chan'), may hold values from -0.078125 to 0.078125
- cotangent: bfloat16 [8, 256, 512], P('sample', 'chan'), may hold values from -0.09375 to 0.09375
Outputs:
- second_out: bfloat16 [8, 256, 512], P('sample', 'chan')
- first_grad: float32 [256, 27, 256], P('chan', None, 'sample')
- second_grad: float32 [256, 27, 256], P('chan', None, 'sample')
All inputs are finite; a program needn't handle non-finite values.
Results may differ from a plain program's by a relative error of at most 0.0061.
Values may be sent and summed in bfloat16 or wider, within the bound.
No kernel may reach another device: no remote copies, remote signals or barrier semaphores. Data moves between devices by JAX's collectives and lax.ppermute only.
A program may use at most 128 MiB of HBM per device.

v0:
```python
import jax
import jax.numpy as jnp
from jax import lax
from jax.sharding import PartitionSpec as P

SIDE = 8


def shifted(fields):
    batch_size, channels = (fields.shape[0], fields.shape[1])
    cube_form = fields.reshape(batch_size, channels, SIDE, SIDE, SIDE)
    padded = jnp.pad(cube_form, ((0, 0), (0, 0), (1, 1), (1, 1), (1, 1)))
    shifted_views = []
    for tap_index in range(27):
        shift_depth, shift_rows, shift_cols = (tap_index // 9, tap_index // 3 % 3, tap_index % 3)
        shifted_views.append(
            padded[
                :,
                :,
                shift_depth : shift_depth + SIDE,
                shift_rows : shift_rows + SIDE,
                shift_cols : shift_cols + SIDE,
            ]
        )
    return jnp.stack(shifted_views, axis=2).reshape(batch_size, channels * 27, SIDE * SIDE * SIDE)


def spread(terms):
    batch_size, channels = (terms.shape[0], terms.shape[1] // 27)
    cube_form = terms.reshape(batch_size, channels, 27, SIDE, SIDE, SIDE)
    padded = jnp.pad(cube_form, ((0, 0), (0, 0), (0, 0), (1, 1), (1, 1), (1, 1)))
    total = jnp.zeros((batch_size, channels, SIDE, SIDE, SIDE), jnp.float32)
    for tap_index in range(27):
        shift_depth, shift_rows, shift_cols = (tap_index // 9, tap_index // 3 % 3, tap_index % 3)
        total = (
            total
            + padded[
                :,
                :,
                tap_index,
                2 - shift_depth : 2 - shift_depth + SIDE,
                2 - shift_rows : 2 - shift_rows + SIDE,
                2 - shift_cols : 2 - shift_cols + SIDE,
            ]
        )
    return total.reshape(batch_size, channels, SIDE * SIDE * SIDE)


def layer_sums(kernel_rows, patches):
    partial_value = jnp.einsum(
        "kc,bkp->bcp", kernel_rows, patches, preferred_element_type=jnp.float32
    )
    return lax.psum_scatter(partial_value, "chan", scatter_dimension=1, tiled=True)


def all_channels(grad_maps):
    return lax.all_gather(grad_maps, "chan", axis=1, tiled=True)


def body(snapshots, first_weight, second_weight, cotangent):
    channel_maps = lax.all_to_all(snapshots, "chan", split_axis=1, concat_axis=2, tiled=True)
    input_patches = shifted(channel_maps)
    first_rows = first_weight.reshape(-1, first_weight.shape[2])
    second_rows = second_weight.reshape(-1, second_weight.shape[2])
    first_sum = layer_sums(first_rows, input_patches)
    first_map = first_sum.astype(jnp.bfloat16)
    first_values = first_map.astype(jnp.float32)
    hidden = jax.nn.silu(first_values).astype(jnp.bfloat16)
    hidden_patches = shifted(hidden)
    second_out = layer_sums(second_rows, hidden_patches).astype(jnp.bfloat16)
    full_cotangent = all_channels(cotangent)
    second_term = jnp.einsum(
        "bkp,bcp->kc", hidden_patches, full_cotangent, preferred_element_type=jnp.float32
    )
    terms = jnp.einsum(
        "kc,bcp->bkp", second_rows, full_cotangent, preferred_element_type=jnp.float32
    )
    hidden_grad = spread(terms)
    sigmoid_values = jax.nn.sigmoid(first_values)
    first_map_grad = (
        hidden_grad * sigmoid_values * (1.0 + first_values * (1.0 - sigmoid_values))
    ).astype(jnp.bfloat16)
    full_map_grad = all_channels(first_map_grad)
    first_term = jnp.einsum(
        "bkp,bcp->kc", input_patches, full_map_grad, preferred_element_type=jnp.float32
    )
    first_grad, second_grad = (
        lax.psum_scatter(first_term, "sample", scatter_dimension=1, tiled=True),
        lax.psum_scatter(second_term, "sample", scatter_dimension=1, tiled=True),
    )
    return (
        second_out,
        first_grad.reshape(first_weight.shape[0], 27, -1),
        second_grad.reshape(second_weight.shape[0], 27, -1),
    )


def solution(mesh):
    placed = (
        P("sample", None, "chan"),
        P("chan", None, None),
        P("chan", None, None),
        P("sample", "chan", None),
    )
    return jax.shard_map(
        body,
        mesh=mesh,
        in_specs=placed,
        out_specs=(P("sample", "chan", None), P("chan", None, "sample"), P("chan", None, "sample")),
        check_vma=False,
    )
```

profile of v0, /device:TPU:0, one launch (start us, length us, event | category | flops | bytes accessed | tf_op | source)
XLA Modules:
  0.0 640.3 jit_solution(11114681304338015524)
XLA Ops:
  7.2 1.0 copy.72
  8.7 1.0 reduce.22
  10.3 6.3 all-to-all-start
  16.7 1.7 copy.63
  18.3 1.2 reshape.411
  19.5 14.5 %all_gather.6 = bf16[1,256,512]{2,1,0:T(8,128)(2,1)S(1)} all-gather(bf16[1,64,512]{2,1,0:T(8,128)(2,1)S(1)} %copy-done.4), channel_id=1, replica_groups=mesh['sample'=8,'chan'=4] {'chan'}, dimensions={1}, use_global_device_ids=true | all-gather | bytes 327680 | tf_op jit(solution)/shard_map/all_gather | solution.py:57
  34.0 0.7 copy-done.1
  34.7 1.8 convolution_bitcast_fusion
  36.5 3.1 copy.65
  39.6 22.4 %reshape.413 = f32[1,64,27,8,8,8]{2,1,5,4,3,0:T(8,128)} reshape(f32[1,1728,512]{1,2,0:T(8,128)} %copy.65) | data formatting | bytes 7077888 | tf_op jit(solution)/shard_map/reshape | solution.py:30
  62.0 178.1 %fusion.16 = (f32[64,8,8,8]{0,3,2,1:T(8,128)S(1)}, f32[64,8,8,8]{0,3,2,1:T(8,128)S(1)}, f32[64,8,8,8]{0,3,2,1:T(8,128)S(1)}, f32[64,8,8,8]{0,3,2,1:T(8,128)S(1)}...) fusion(f32[1,64,27,8,8,8]{2,1,5,4,3,0:T(8,128)} %reshape.413), kind=kLoop, calls=%fused_computation.42 | loop fusion | flops 524288 | bytes 34996224 | tf_op jit(solution)/shard_map/slice | solution.py:37
  240.6 1.2 reshape.408
  243.1 0.9 reshape.443
  244.1 0.7 fusion.40
  245.5 0.7 fusion.44
  247.5 0.7 fusion.50
  248.2 0.7 fusion.52
  249.6 0.7 fusion.56
  250.3 0.7 fusion.58
  251.6 0.7 fusion.62
  252.3 0.7 fusion.64
  253.7 0.7 fusion.66
  254.4 0.7 fusion.68
  255.7 0.7 fusion.72
  256.4 0.7 fusion.74
  257.8 0.7 fusion.78
  258.5 0.7 fusion.80
  259.9 0.7 fusion.84
  260.5 0.7 fusion.86
  261.9 0.7 fusion.90
  262.6 9.5 %copy.58 = bf16[1,64,27,8,8,8]{2,1,5,4,3,0:T(8,128)(2,1)} copy(bf16[1,64,27,8,8,8]{1,5,4,3,2,0:T(8,128)(2,1)} %fusion.90) | data formatting | bytes 3538944 | tf_op jit(solution)/shard_map/stack | solution.py:25
  272.1 11.3 %reshape.407 = bf16[1728,512]{0,1:T(8,128)(2,1)S(1)} reshape(bf16[1,64,27,8,8,8]{2,1,5,4,3,0:T(8,128)(2,1)} %copy.58) | data formatting | bytes 3538944 | tf_op jit(solution)/shard_map/reshape.2
  283.4 2.6 convolution_bitcast_fusion.2
  286.0 1.3 copy.60
  287.3 140.8 %all-reduce.7 = bf16[1,256,512]{2,0,1:T(2,128)(2,1)} all-reduce(f32[1,256,512]{2,0,1:T(1,128)S(1)} %copy.60), channel_id=2, replica_groups=mesh['sample'=8,'chan'=4] {'chan'}, use_global_device_ids=true, to_apply=%region_0.1.clone | all-reduce | flops 131072 | bytes 786432
  428.1 1.0 constant_dynamic-slice_fusion
  429.3 1.6 fusion.33
  430.9 0.7 fusion.92
  432.3 0.7 fusion.96
  434.3 0.7 fusion.102
  435.1 14.1 %all_gather.7 = bf16[1,256,512]{2,1,0:T(8,128)(2,1)S(1)} all-gather(bf16[1,64,512]{2,1,0:T(8,128)(2,1)S(1)} %copy.66), channel_id=1, replica_groups=mesh['sample'=8,'chan'=4] {'chan'}, dimensions={1}, use_global_device_ids=true | all-gather | bytes 327680 | tf_op jit(solution)/shard_map/all_gather | solution.py:57
  449.2 2.0 fusion.34
  451.3 0.7 fusion.104
  452.7 0.7 fusion.108
  453.3 0.7 fusion.110
  454.7 0.7 fusion.114
  455.4 0.7 fusion.116
  456.8 0.7 fusion.118
  457.4 0.7 fusion.120
  458.8 0.7 fusion.124
  459.5 0.7 fusion.126
  460.9 0.7 fusion.130
  461.6 0.7 fusion.132
  462.9 0.7 fusion.136
  463.6 0.7 fusion.138
  465.0 0.7 fusion.142
  465.7 9.6 %copy.62 = bf16[1,64,27,8,8,8]{2,1,5,4,3,0:T(8,128)(2,1)} copy(bf16[1,64,27,8,8,8]{1,5,4,3,2,0:T(8,128)(2,1)} %fusion.142) | data formatting | bytes 3538944 | tf_op jit(solution)/shard_map/stack | solution.py:25
  475.2 11.3 %reshape.410 = bf16[1728,512]{0,1:T(8,128)(2,1)S(1)} reshape(bf16[1,64,27,8,8,8]{2,1,5,4,3,0:T(8,128)(2,1)} %copy.62) | data formatting | bytes 3538944 | tf_op jit(solution)/shard_map/reshape.5
  486.6 1.9 fusion.37
  489.6 136.3 %all-reduce.8 = bf16[1,256,512]{2,0,1:T(2,128)(2,1)S(1)} all-reduce(f32[1,256,512]{2,0,1:T(1,128)S(1)} %copy.64), channel_id=3, replica_groups=mesh['sample'=8,'chan'=4] {'chan'}, use_global_device_ids=true, to_apply=%region_1.2.clone | all-reduce | flops 131072 | bytes 786432
  626.7 2.2 reshape.415
  628.9 1.2 copy.68
  630.1 2.2 reshape.416
  632.3 1.2 copy.69
  (50 shorter events, 18.0 us)
Async XLA Ops:
  7.2 12.4 %copy-start.4 = (bf16[1,64,512]{2,1,0:T(8,128)(2,1)S(1)}, bf16[1,64,512]{2,1,0:T(8,128)(2,1)}, u32[]{:S(2)}) copy-start(bf16[1,64,512]{2,1,0:T(8,128)(2,1)} %param.7) | copy-start | bytes 196612
  10.3 232.7 %all-to-all-start = ((bf16[4,2,4096]{2,1,0:T(2,128)(2,1)}), bf16[4,2,4096]{2,1,0:T(2,128)(2,1)}, u32[]{:S(2)}, u32[]{:S(2)}) async-start(bf16[4,2,4096]{2,1,0:T(2,128)(2,1)} %reshape.442), calls=%async_computation | async-start | bytes 131072 | tf_op jit(solution)/shard_map/all_to_all | solution.py:61
  16.6 610.1 %reduce-scatter.3.cloned.1.call-start = ((), (), s32[]{:S(2)}) async-start(), calls=%async_computation.3 | async-start | bytes 2064384 | tf_op jit(solution)/shard_map/reduce_scatter | solution.py:88
  34.0 0.7 copy-start.1
  62.0 178.1 %copy-start.3 = (bf16[64,27,256]{2,0,1:T(8,128)(2,1)S(1)}, bf16[64,27,256]{2,0,1:T(8,128)(2,1)}, u32[]{:S(2)}) copy-start(bf16[64,27,256]{2,0,1:T(8,128)(2,1)} %param.5) | copy-start | bytes 2654212
  240.1 1.7 copy-start.5
  451.2 178.8 %reduce-scatter.5.cloned.1.call-start = ((), (), s32[]{:S(2)}) async-start(), calls=%async_computation.4 | async-start | bytes 2064384 | tf_op jit(solution)/shard_map/reduce_scatter | solution.py:89
  475.2 11.4 %copy-start.2 = (bf16[1,256,512]{2,1,0:T(8,128)(2,1)S(1)}, bf16[1,256,512]{2,1,0:T(8,128)(2,1)}, u32[]{:S(2)}) copy-start(bf16[1,256,512]{2,1,0:T(8,128)(2,1)} %copy-done.1) | copy-start | bytes 786436
  486.6 1.9 copy-start
Sparse Core Ops, SparseCore 0:
  451.4 40.2 reduce-scatter.2
  495.0 39.6 reduce-scatter.4
where the time goes:
time: 642 us; the launch traced here: 640 us
  blocking collectives  306 us (48%)
  other arithmetic  181 us (28%)
  local copies, waits for them, and re-layouts  124 us (19%)
  between operations  14.9 us (2%)
  matrix products  8.92 us (1%)
    unnamed x2, blocking collectives  277 us
    slice x1, other arithmetic, spread(): padded[:, :, tap_index, 2 - shift_depth:2 - shift_depth + SIDE, 2 - shift...  178 us
    unnamed x76, local copies, waits for them, and re-layouts  46.2 us
    all_gather x2, blocking collectives, all_channels(): return lax.all_gather(grad_maps, 'chan', axis=1, tiled=True)  28.6 us
    another operation x2, local copies, waits for them, and re-layouts  22.6 us
    reshape x1, local copies, waits for them, and re-layouts, spread(): cube_form = terms.reshape(batch_size, channels, 27, SIDE, SIDE, SIDE)  22.4 us
    another operation x4, local copies, waits for them, and re-layouts, shifted(): jnp.stack(shifted_views, axis=2)  20.4 us
  transfers between devices with their start and end apart: 3, of which 0 were waited for; matrix products, arithmetic and copies ran while one was open for 39% of the time, Pallas kernels for 0%

commit v1 on v0

--- a/solution.py
+++ b/solution.py
@@ -4,6 +4,17 @@
 from jax.sharding import PartitionSpec as P
 
 SIDE = 8
+
+
+def gather_around(x, axis, dim):
+    ways = lax.axis_size(axis)
+    pieces = [x]
+    for far in range(1, ways):
+        pieces.append(
+            lax.ppermute(pieces[far - 1], axis, [(d, (d - 1) % ways) for d in range(ways)])
+        )
+    line = jnp.concatenate(pieces, axis=dim)
+    return jnp.roll(line, lax.axis_index(axis) * x.shape[dim], axis=dim)
 
 
 def shifted(fields):
@@ -54,7 +65,7 @@
 
 
 def all_channels(grad_maps):
-    return lax.all_gather(grad_maps, "chan", axis=1, tiled=True)
+    return gather_around(grad_maps, "chan", 1)
 
 
 def body(snapshots, first_weight, second_weight, cotangent):

time: 642 us -> 622 us (0.969)
  blocking collectives: 306 us -> 278 us
  local copies, waits for them, and re-layouts: 124 us -> 103 us
  starting transfers between devices: 6.36 us -> 24.5 us
  waiting for transfers between devices: 0.04 us -> 11.3 us
    all_gather x2 -> x0, blocking collectives: 28.6 us -> none  [all_channels(): return lax.all_gather(grad_maps, 'chan', axis=1, tiled=True)]
    ppermute x0 -> x6, starting transfers between devices: none -> 18.1 us  [gather_around(): lax.ppermute(pieces[far - 1], axis, [(d, (d - 1) % ways) for d in range(w...]
    unnamed x76 -> x82, local copies, waits for them, and re-layouts: 46.2 us -> 29.2 us
    ppermute x0 -> x6, waiting for transfers between devices: none -> 11.2 us  [gather_around(): lax.ppermute(pieces[far - 1], axis, [(d, (d - 1) % ways) for d in range(w...]
  transfers between devices with their start and end apart: 3 -> 9, of which waited for: 0 -> 4; matrix products, arithmetic and copies ran while one was open for 39% -> 9% of each run, Pallas kernels for 0% -> 0%
where the time goes in v1:
time: 622 us; the launch traced here: 621 us
  blocking collectives  278 us (45%)
  other arithmetic  180 us (29%)
  local copies, waits for them, and re-layouts  103 us (17%)
  starting transfers between devices  24.5 us (4%)
  between operations  15 us (2%)
  waiting for transfers between devices  11.3 us (2%)
  matrix products  9.42 us (2%)
    unnamed x2, blocking collectives  278 us
    slice x1, other arithmetic, spread(): padded[:, :, tap_index, 2 - shift_depth:2 - shift_depth + SIDE, 2 - shift...  177 us
    unnamed x82, local copies, waits for them, and re-layouts  29.2 us
    another operation x2, local copies, waits for them, and re-layouts  22.6 us
    reshape x1, local copies, waits for them, and re-layouts, spread(): cube_form = terms.reshape(batch_size, channels, 27, SIDE, SIDE, SIDE)  22.4 us
    ppermute x6, starting transfers between devices, gather_around(): lax.ppermute(pieces[far - 1], axis, [(d, (d - 1) % ways) for d in range(w...  18.1 us
    another operation x4, local copies, waits for them, and re-layouts, shifted(): jnp.stack(shifted_views, axis=2)  17.6 us
  transfers between devices with their start and end apart: 9, of which 4 were waited for; matrix products, arithmetic and copies ran while one was open for 9% of the time, Pallas kernels for 0%

profile of v1, /device:TPU:0, one launch (start us, length us, event | category | flops | bytes accessed | tf_op | source)
XLA Modules:
  0.0 621.5 jit_solution(8211519301164974273)
XLA Ops:
  7.2 1.0 copy.71
  8.7 1.0 reduce.22
  9.7 0.6 reshape.442
  10.4 6.3 %all-to-all-start = ((bf16[4,2,4096]{2,1,0:T(2,128)(2,1)}), bf16[4,2,4096]{2,1,0:T(2,128)(2,1)S(1)}, u32[]{:S(2)}, u32[]{:S(2)}) async-start(bf16[4,2,4096]{2,1,0:T(2,128)(2,1)} %reshape.442), calls=%async_computation | async-start | bytes 131072 | tf_op jit(solution)/shard_map/all_to_all | solution.py:72
  16.7 3.8 collective-permute-start
  20.5 1.7 copy.63
  22.2 1.2 reshape.411
  25.5 1.3 collective-permute-start.1
  27.0 0.7 fusion.54
  27.7 0.7 fusion.56
  28.4 0.7 fusion.58
  29.1 0.7 fusion.60
  29.7 0.7 fusion.62
  30.4 0.7 fusion.64
  31.1 0.7 fusion.66
  31.8 0.7 fusion.68
  32.5 0.7 fusion.70
  33.2 0.7 fusion.72
  33.9 0.7 fusion.74
  34.5 0.7 fusion.76
  35.2 0.7 fusion.78
  35.9 0.7 constant_dynamic-update-slice_fusion
  36.6 0.7 fusion.80
  37.3 0.7 fusion.82
  38.0 0.7 fusion.84
  38.6 0.7 fusion.86
  39.3 0.7 fusion.88
  40.0 0.7 fusion.90
  40.7 0.7 fusion.92
  41.4 0.7 fusion.94
  42.1 0.7 fusion.96
  42.8 0.7 fusion.98
  43.4 0.7 fusion.100
  44.1 0.7 fusion.102
  44.8 0.7 fusion.104
  45.5 9.5 %copy.58 = bf16[1,64,27,8,8,8]{2,1,5,4,3,0:T(8,128)(2,1)} copy(bf16[1,64,27,8,8,8]{1,5,4,3,2,0:T(8,128)(2,1)} %fusion.104) | data formatting | bytes 3538944 | tf_op jit(solution)/shard_map/stack | solution.py:36
  55.0 11.3 %reshape.407 = bf16[1728,512]{0,1:T(8,128)(2,1)S(1)} reshape(bf16[1,64,27,8,8,8]{2,1,5,4,3,0:T(8,128)(2,1)} %copy.58) | data formatting | bytes 3538944 | tf_op jit(solution)/shard_map/reshape.2
  66.3 1.2 copy-done.3
  68.6 141.7 %all-reduce.7 = bf16[1,256,512]{2,0,1:T(2,128)(2,1)S(1)} all-reduce(f32[1,256,512]{2,0,1:T(1,128)S(1)} %copy.60), channel_id=2, replica_groups=mesh['sample'=8,'chan'=4] {'chan'}, use_global_device_ids=true, to_apply=%region_0.1.clone | all-reduce | flops 131072 | bytes 786432
  210.3 1.3 collective-permute-start.2
  211.8 0.8 copy.61
  212.6 2.0 collective-permute-done.2
  214.6 1.4 fusion.49
  216.0 0.7 copy-done.1
  216.7 1.8 convolution_bitcast_fusion
  218.5 3.3 copy.65
  221.8 22.4 %reshape.413 = f32[1,64,27,8,8,8]{2,1,5,4,3,0:T(8,128)} reshape(f32[1,1728,512]{1,2,0:T(8,128)} %copy.65) | data formatting | bytes 7077888 | tf_op jit(solution)/shard_map/reshape | solution.py:41
  244.2 176.8 %fusion.16 = (f32[64,8,8,8]{0,3,2,1:T(8,128)S(1)}, f32[64,8,8,8]{0,3,2,1:T(8,128)S(1)}, f32[64,8,8,8]{0,3,2,1:T(8,128)S(1)}, f32[64,8,8,8]{0,3,2,1:T(8,128)S(1)}...) fusion(f32[1,64,27,8,8,8]{2,1,5,4,3,0:T(8,128)} %reshape.413), kind=kLoop, calls=%fused_computation.42 | loop fusion | flops 524288 | bytes 34996224 | tf_op jit(solution)/shard_map/slice | solution.py:48
  421.0 0.9 fusion.33
  423.3 7.4 %copy.62 = bf16[1,64,27,8,8,8]{2,1,5,4,3,0:T(8,128)(2,1)} copy(bf16[1,64,27,8,8,8]{1,5,4,3,2,0:T(8,128)(2,1)S(1)} %fusion.156) | data formatting | bytes 3538944 | tf_op jit(solution)/shard_map/stack | solution.py:36
  430.7 11.3 %reshape.410 = bf16[1728,512]{0,1:T(8,128)(2,1)S(1)} reshape(bf16[1,64,27,8,8,8]{2,1,5,4,3,0:T(8,128)(2,1)} %copy.62) | data formatting | bytes 3538944 | tf_op jit(solution)/shard_map/reshape.5
  442.1 1.9 fusion.159
  444.0 3.1 collective-permute-start.3
  447.2 3.6 collective-permute-done.3
  450.8 4.3 collective-permute-start.4
  455.1 3.0 collective-permute-done.4
  458.1 4.3 collective-permute-start.5
  462.4 2.5 collective-permute-done.5
  464.9 4.5 fusion.39
  470.5 136.6 %all-reduce.8 = bf16[1,256,512]{2,0,1:T(2,128)(2,1)S(1)} all-reduce(f32[1,256,512]{2,0,1:T(1,128)S(1)} %copy.64), channel_id=3, replica_groups=mesh['sample'=8,'chan'=4] {'chan'}, use_global_device_ids=true, to_apply=%region_1.2.clone | all-reduce | flops 131072 | bytes 786432
  607.9 2.2 reshape.416
  610.0 1.2 copy.68
  611.3 2.2 reshape.415
  613.4 1.2 copy.67
  (66 shorter events, 6.5 us)
Async XLA Ops:
  7.2 16.3 %copy-start.4 = (bf16[64,27,256]{2,0,1:T(8,128)(2,1)S(1)}, bf16[64,27,256]{2,0,1:T(8,128)(2,1)}, u32[]{:S(2)}) copy-start(bf16[64,27,256]{2,0,1:T(8,128)(2,1)} %param.7) | copy-start | bytes 2654212
  10.4 16.4 %all-to-all-start = ((bf16[4,2,4096]{2,1,0:T(2,128)(2,1)}), bf16[4,2,4096]{2,1,0:T(2,128)(2,1)S(1)}, u32[]{:S(2)}, u32[]{:S(2)}) async-start(bf16[4,2,4096]{2,1,0:T(2,128)(2,1)} %reshape.442), calls=%async_computation | async-start | bytes 131072 | tf_op jit(solution)/shard_map/all_to_all | solution.py:72
  16.7 591.2 %reduce-scatter.5.cloned.1.call-start = ((), (), s32[]{:S(2)}) async-start(), calls=%async_computation.4 | async-start | bytes 2064384 | tf_op jit(solution)/shard_map/reduce_scatter | solution.py:100
  16.7 8.8 %collective-permute-start = (bf16[1,64,512]{2,1,0:T(8,128)(2,1)}, bf16[1,64,512]{2,1,0:T(8,128)(2,1)S(1)}, u32[]{:S(2)}, u32[]{:S(2)}) collective-permute-start(bf16[1,64,512]{2,1,0:T(8,128)(2,1)} %param.9), channel_id=1, source_target_pairs={{0,3},{1,0},{2,1},{3,2},{4,7},{5,4},{6,5},{7,6},{8,11},{9,8},{10,9... | collective-permute-start | bytes 196616 | tf_op jit(solution)/shard_map/ppermute | solution.py:14
  20.5 3.8 copy-start.8
  25.5 184.8 %collective-permute-start.1 = (bf16[1,64,512]{2,1,0:T(8,128)(2,1)S(1)}, bf16[1,64,512]{2,1,0:T(8,128)(2,1)S(1)}, u32[]{:S(2)}, u32[]{:S(2)}) collective-permute-start(bf16[1,64,512]{2,1,0:T(8,128)(2,1)S(1)} %collective-permute-done), channel_id=1, source_target_pairs={{0,3},{1,0},{2,1},{3,2},{4,7},{5,4},{6,5},{7,6},{8,11},{9,8},{10,9... | collective-permute-start | bytes 196616 | tf_op jit(solution)/shard_map/ppermute | solution.py:14
  66.3 1.2 copy-start.3
  67.5 147.1 %copy-start.7 = (bf16[1,64,512]{2,1,0:T(8,128)(2,1)S(1)}, bf16[1,64,512]{2,1,0:T(8,128)(2,1)}, u32[]{:S(2)}) copy-start(bf16[1,64,512]{2,1,0:T(8,128)(2,1)} %param.9) | copy-start | bytes 196612
  210.3 4.3 collective-permute-start.2
  216.0 0.7 copy-start.1
  244.2 176.8 %copy-start.5 = (bf16[1,64,512]{1,2,0:T(8,128)(2,1)S(1)}, bf16[1,64,512]{1,2,0:T(8,128)(2,1)}, u32[]{:S(2)}) copy-start(bf16[1,64,512]{1,2,0:T(8,128)(2,1)} %copy.61) | copy-start | bytes 196612
  430.7 11.4 %copy-start.2 = (bf16[256,512]{1,0:T(8,128)(2,1)S(1)}, bf16[256,512]{1,0:T(8,128)(2,1)}, u32[]{:S(2)}) copy-start(bf16[256,512]{1,0:T(8,128)(2,1)} %copy-done.1) | copy-start | bytes 786436
  442.1 2.0 copy-start.6
  444.0 167.3 %reduce-scatter.3.cloned.1.call-start = ((), (), s32[]{:S(2)}) async-start(), calls=%async_computation.3 | async-start | bytes 2064384 | tf_op jit(solution)/shard_map/reduce_scatter | solution.py:99
  444.0 25.4 %copy-start = (bf16[1728,256]{1,0:T(8,128)(2,1)S(1)}, bf16[1728,256]{1,0:T(8,128)(2,1)}, u32[]{:S(2)}) copy-start(bf16[1728,256]{1,0:T(8,128)(2,1)} %reshape.411) | copy-start | bytes 2654212
  444.0 6.8 %collective-permute-start.3 = (bf16[1,64,512]{1,2,0:T(8,128)(2,1)S(1)}, bf16[1,64,512]{1,2,0:T(8,128)(2,1)S(1)}, u32[]{:S(2)}, u32[]{:S(2)}) collective-permute-start(bf16[1,64,512]{1,2,0:T(8,128)(2,1)S(1)} %copy-done.6), channel_id=1, source_target_pairs={{0,3},{1,0},{2,1},{3,2},{4,7},{5,4},{6,5},{7,6},{8,11},{9,8},{10,9... | collective-permute-start | bytes 196616 | tf_op jit(solution)/shard_map/ppermute | solution.py:14
  450.8 7.3 %collective-permute-start.4 = (bf16[1,64,512]{1,2,0:T(8,128)(2,1)S(1)}, bf16[1,64,512]{1,2,0:T(8,128)(2,1)S(1)}, u32[]{:S(2)}, u32[]{:S(2)}) collective-permute-start(bf16[1,64,512]{1,2,0:T(8,128)(2,1)S(1)} %collective-permute-done.3), channel_id=1, source_target_pairs={{0,3},{1,0},{2,1},{3,2},{4,7},{5,4},{6,5},{7,6},{8,11},{9,8},{10,9... | collective-permute-start | bytes 196616 | tf_op jit(solution)/shard_map/ppermute | solution.py:14
  458.1 6.8 %collective-permute-start.5 = (bf16[1,64,512]{1,2,0:T(8,128)(2,1)S(1)}, bf16[1,64,512]{1,2,0:T(8,128)(2,1)S(1)}, u32[]{:S(2)}, u32[]{:S(2)}) collective-permute-start(bf16[1,64,512]{1,2,0:T(8,128)(2,1)S(1)} %collective-permute-done.4), channel_id=1, source_target_pairs={{0,3},{1,0},{2,1},{3,2},{4,7},{5,4},{6,5},{7,6},{8,11},{9,8},{10,9... | collective-permute-start | bytes 196616 | tf_op jit(solution)/shard_map/ppermute | solution.py:14
Sparse Core Ops, SparseCore 0:
  444.1 40.4 reduce-scatter.4
  487.9 39.6 reduce-scatter.2
